TPU v7x, 128 devices: a whole 4x4x4 slice. The times are simulated.
128 devices in a mesh: expert: 32 (over y, x, core), dp: 4 (over z).
Axes of the slice: x: 4, y: 4, z: 4, core: 2. Of those that a mesh axis runs over, the one named last changes fastest.
Arguments:
- tokens: bfloat16 [4096, 4096], P('expert', 'dp'), may hold values from -6 to 6
- cotangent: bfloat16 [4096, 4096], P('expert', 'dp'), may hold values from -6 to 6
- gate_probs: bfloat16 [4096, 8], P('expert'), may hold values from 0.019897461 to 0.3984375
- expert_ids: int32 [4096, 8], P('expert'), may hold values from 0 to 31, all different within a row; in each aligned block of 128 rows (0 to 127, 128 to 255, ...) at most 36 rows name the same one
- gate_weight: bfloat16 [32, 4096, 1024], P('expert', 'dp'), may hold values from -0.09375 to 0.09375
- up_weight: bfloat16 [32, 4096, 1024], P('expert', 'dp'), may hold values from -0.09375 to 0.09375
- down_weight: bfloat16 [32, 1024, 4096], P('expert', None, 'dp'), may hold values from -0.1875 to 0.1875
Outputs:
- grad_tokens: bfloat16 [4096, 4096], P('expert', 'dp')
- grad_gates: float32 [4096, 8], P('expert')
- grad_gate_weight: float32 [32, 4096, 1024], P('expert', 'dp')
- grad_up_weight: float32 [32, 4096, 1024], P('expert', 'dp')
- grad_down_weight: float32 [32, 1024, 4096], P('expert', None, 'dp')
Inputs may be any that keep to these rules, and one draw needn't show every extreme that they name: `expert_ids`: each row names 8 different experts. Among the 128 rows of one group no expert is named more than 36 times, and in every draw some expert is named exactly 36 times by the rows of some group.
All inputs are finite; a program needn't handle non-finite values.
Results may differ from a plain program's by a relative error of at most 0.012.
Values may be sent and summed in bfloat16 or wider, within the bound.
A program may use at most 128 MiB of HBM per device.

v0:
```python
import jax
import jax.numpy as jnp
from jax import lax
from jax.sharding import PartitionSpec as P

TOP = 8
EXPERTS = 32
CAP = 36


def local_slots(expert_ids):
    flat_ids = expert_ids.reshape(-1)
    columns = jnp.arange(EXPERTS, dtype=jnp.int32)
    member = (flat_ids[:, None] == columns[None, :]).astype(jnp.int32)
    ranked = jnp.cumsum(member, axis=0) - 1
    within = jnp.sum(member * ranked, axis=1)
    return flat_ids * CAP + within


def pack_rows(tokens, cotangent, gate_probs, target):
    token_count = tokens.shape[0]
    slot_total = EXPERTS * CAP
    slot_index = jnp.arange(slot_total, dtype=jnp.int32)
    placed = target[None, :] == slot_index[:, None]
    chosen = jnp.any(placed.reshape(slot_total, token_count, TOP), axis=2).astype(jnp.bfloat16)
    x_send = jnp.dot(chosen, tokens, preferred_element_type=jnp.float32).astype(jnp.bfloat16)
    dy_send = jnp.dot(chosen, cotangent, preferred_element_type=jnp.float32).astype(jnp.bfloat16)
    weights_flat = gate_probs.reshape(-1).astype(jnp.float32)
    g_send = jnp.sum(jnp.where(placed, weights_flat[None, :], 0.0), axis=1).astype(jnp.bfloat16)
    return (x_send, dy_send, g_send)


def hidden_units(gate_pre, up_pre, back_hidden, g_rows):
    sigmoid_gate = jax.nn.sigmoid(gate_pre)
    swish_gate = gate_pre * sigmoid_gate
    hidden = (swish_gate * up_pre).astype(jnp.bfloat16)
    product = back_hidden * hidden.astype(jnp.float32)
    grad_hidden = g_rows * back_hidden
    derivative = sigmoid_gate * (1.0 + gate_pre * (1.0 - sigmoid_gate))
    grad_gate_pre = (grad_hidden * up_pre * derivative).astype(jnp.bfloat16)
    grad_up_pre = (grad_hidden * swish_gate).astype(jnp.bfloat16)
    return (hidden, grad_gate_pre, grad_up_pre, product)


def shards(tokens, cotangent, gate_probs, expert_ids, gate_weight, up_weight, down_weight):
    expert_count = lax.axis_size("expert")
    data_count = lax.axis_size("dp")
    local_count = gate_weight.shape[0]
    width_part = tokens.shape[1]
    token_count = tokens.shape[0]
    target = local_slots(expert_ids)
    x_send, dy_send, g_send = pack_rows(tokens, cotangent, gate_probs, target)
    x_recv, dy_recv, g_recv = (
        lax.all_to_all(x_send, "expert", split_axis=0, concat_axis=0, tiled=True),
        lax.all_to_all(dy_send, "expert", split_axis=0, concat_axis=0, tiled=True),
        lax.all_to_all(g_send, "expert", split_axis=0, concat_axis=0, tiled=True),
    )
    x_grid = x_recv.reshape(expert_count, local_count, CAP, width_part)
    dy_grid = dy_recv.reshape(expert_count, local_count, CAP, width_part)
    g_grid = g_recv.reshape(expert_count, local_count, CAP)
    g_rows = jnp.transpose(g_grid, (1, 0, 2)).astype(jnp.float32)[..., None]
    gate_part = jnp.einsum(
        "secd,edf->escf", x_grid, gate_weight, preferred_element_type=jnp.float32
    )
    up_part = jnp.einsum("secd,edf->escf", x_grid, up_weight, preferred_element_type=jnp.float32)
    back_part = jnp.einsum(
        "secd,efd->escf", dy_grid, down_weight, preferred_element_type=jnp.float32
    )
    gate_pre, up_pre, back_hidden = (
        lax.psum_scatter(gate_part, "dp", scatter_dimension=3, tiled=True),
        lax.psum_scatter(up_part, "dp", scatter_dimension=3, tiled=True),
        lax.psum_scatter(back_part, "dp", scatter_dimension=3, tiled=True),
    )
    hidden, grad_gate_pre, grad_up_pre, product = hidden_units(
        gate_pre, up_pre, back_hidden, g_rows
    )
    block_sum = jnp.sum(product, axis=3, keepdims=True).astype(jnp.bfloat16)
    hidden_all, gate_grad_all, up_grad_all, gate_blocks = (
        lax.all_gather(hidden, "dp", axis=3, tiled=True),
        lax.all_gather(grad_gate_pre, "dp", axis=3, tiled=True),
        lax.all_gather(grad_up_pre, "dp", axis=3, tiled=True),
        lax.all_gather(block_sum, "dp", axis=3, tiled=True),
    )
    input_terms = jnp.einsum(
        "escf,edf->secd", gate_grad_all, gate_weight, preferred_element_type=jnp.float32
    )
    input_terms = input_terms + jnp.einsum(
        "escf,edf->secd", up_grad_all, up_weight, preferred_element_type=jnp.float32
    )
    input_part = input_terms.astype(jnp.bfloat16).reshape(
        expert_count * local_count * CAP, width_part
    )
    scaled_dy = dy_grid * g_grid[..., None]
    grad_down = jnp.einsum(
        "escf,secd->efd", hidden_all, scaled_dy, preferred_element_type=jnp.float32
    )
    grad_gate = jnp.einsum(
        "secd,escf->edf", x_grid, gate_grad_all, preferred_element_type=jnp.float32
    )
    grad_up = jnp.einsum("secd,escf->edf", x_grid, up_grad_all, preferred_element_type=jnp.float32)
    block_send = jnp.transpose(gate_blocks, (1, 0, 2, 3)).reshape(
        expert_count * local_count * CAP, data_count
    )
    input_table, gate_table = (
        lax.all_to_all(input_part, "expert", split_axis=0, concat_axis=0, tiled=True),
        lax.all_to_all(block_send, "expert", split_axis=0, concat_axis=0, tiled=True),
    )
    picked = jnp.take(input_table, target, axis=0).astype(jnp.float32)
    grad_tokens = picked.reshape(token_count, TOP, width_part).sum(1).astype(jnp.bfloat16)
    grad_gates = (
        jnp.take(gate_table, target, axis=0).astype(jnp.float32).sum(1).reshape(token_count, TOP)
    )
    return (grad_tokens, grad_gates, grad_gate, grad_up, grad_down)


def solution(mesh):
    placed = (
        P("expert", "dp"),
        P("expert", "dp"),
        P("expert", None),
        P("expert", None),
        P("expert", "dp", None),
        P("expert", "dp", None),
        P("expert", None, "dp"),
    )
    return jax.shard_map(
        shards,
        mesh=mesh,
        in_specs=placed,
        out_specs=(
            P("expert", "dp"),
            P("expert", None),
            P("expert", "dp", None),
            P("expert", "dp", None),
            P("expert", None, "dp"),
        ),
        check_vma=False,
    )
```

profile of v0, /device:TPU:1, one launch (start us, length us, event | category | flops | bytes accessed | tf_op | source)
XLA Modules:
  0.0 405.3 jit_solution(17590556254104163297)
XLA Ops:
  7.2 0.9 copy.58
  8.2 0.1 eq.46
  8.2 0.1 reshape.206
  8.4 9.0 %reduce-window.6 = s32[32,8,128]{2,1,0:T(8,128)S(1)} reduce-window(s32[32,8,128]{2,1,0:T(8,128)S(1)} %fusion.37, s32[]{:T(128)} %constant.25.clone.1), window={size=1x1x128 pad=0_0x0_0x127_0}, to_apply=%region_0.0 | reduce-window | flops 4161536 | bytes 262148 | tf_op jit(solution)/shard_map/reduce-window
  17.4 0.1 slice.12
  17.5 0.1 copy.60
  17.6 0.1 copy.61
  17.7 0.1 add_add_fusion
  17.9 0.1 reduce_sum.53
  18.0 0.7 compare_and_fusion.1
  18.7 4.2 %fusion = pred[1152,128]{1,0:T(8,128)(4,1)S(1)} fusion(s32[128,8]{0,1:T(8,128)S(1)} %get-tuple-element.35), kind=kLoop, calls=%fused_computation.6 | loop fusion | flops 2211840 | bytes 151552 | tf_op jit(solution)/shard_map/reduce_or | solution.py:25
  22.9 3.1 convolution_convert_fusion
  26.0 4.1 %all_to_all.33 = bf16[32,36,1024]{2,1,0:T(8,128)(2,1)} reshape(bf16[1152,1024]{1,0:T(8,128)(2,1)} %convolution_convert_fusion) | data formatting | bytes 4718592 | tf_op jit(solution)/shard_map/all_to_all | solution.py:54
  30.1 42.6 %all_to_all.45 = bf16[32,36,1024]{2,1,0:T(8,128)(2,1)S(1)} all-to-all(bf16[32,36,1024]{2,1,0:T(8,128)(2,1)} %all_to_all.33), channel_id=1, replica_groups=mesh['expert'=32,'dp'=4] {'expert'}, dimensions={0} | all-to-all | bytes 4718592 | tf_op jit(solution)/shard_map/all_to_all | solution.py:54
  72.7 1.5 copy-done.2
  74.2 4.6 %convolution_bitcast_fusion.1 = f32[1,32,36,1024]{3,2,1,0:T(8,128)} fusion(bf16[32,36,1024]{2,1,0:T(8,128)(2,1)S(1)} %all_to_all.45, bf16[1,1024,1024]{2,1,0:T(8,128)(2,1)S(1)} %copy-done), kind=kOutput, calls=%fused_computation.21 | convolution fusion | flops 2415919104 | bytes 9175040 | tf_op jit(solution)/shard_map/secd,edf->escf/dot_general | solution.py:65
  78.8 0.0 reduce-scatter.8.cloned.1.call-start
  78.9 7.6 %convolution_bitcast_fusion = f32[1,32,36,1024]{3,2,1,0:T(8,128)} fusion(bf16[32,36,1024]{2,1,0:T(8,128)(2,1)} %copy-done.2, bf16[1,1024,1024]{2,1,0:T(8,128)(2,1)} %param.11), kind=kOutput, calls=%fused_computation.20 | convolution fusion | flops 2415919104 | bytes 9175040 | tf_op jit(solution)/shard_map/secd,edf->escf/dot_general | solution.py:62
  86.5 0.0 reduce-scatter.4.cloned.1.call-start
  86.6 1.0 copy-done.5
  87.5 2.2 convolution_convert_fusion.1
  89.7 4.1 %all_to_all.31 = bf16[32,36,1024]{2,1,0:T(8,128)(2,1)} reshape(bf16[1152,1024]{1,0:T(8,128)(2,1)} %convolution_convert_fusion.1) | data formatting | bytes 4718592 | tf_op jit(solution)/shard_map/all_to_all | solution.py:55
  93.8 38.4 %all_to_all.46 = bf16[32,36,1024]{2,1,0:T(8,128)(2,1)S(1)} all-to-all(bf16[32,36,1024]{2,1,0:T(8,128)(2,1)} %all_to_all.31), channel_id=1, replica_groups=mesh['expert'=32,'dp'=4] {'expert'}, dimensions={0} | all-to-all | bytes 4718592 | tf_op jit(solution)/shard_map/all_to_all | solution.py:55
  132.2 1.5 copy-done.4
  133.7 4.7 %convolution_bitcast_fusion.2 = f32[1,32,36,1024]{3,2,1,0:T(8,128)} fusion(bf16[32,36,1024]{2,1,0:T(8,128)(2,1)S(1)} %all_to_all.46, bf16[1,1024,1024]{2,1,0:T(8,128)(2,1)S(1)} %copy-done.9), kind=kOutput, calls=%fused_computation.22 | convolution fusion | flops 2415919104 | bytes 9175040 | tf_op jit(solution)/shard_map/secd,efd->escf/dot_general | solution.py:66
  138.4 0.0 all-gather.6.cloned.1.call-start
  138.5 0.6 copy-done.7
  139.1 0.1 copy.64
  139.2 0.1 reshape.215
  139.3 0.6 select_reduce_fusion
  139.8 0.1 convert_element_type.99
  140.0 10.6 %all_to_all.47 = bf16[32,36,1]{1,2,0:T(2,128)(2,1)S(1)} all-to-all(bf16[32,36,1]{1,2,0:T(2,128)(2,1)S(1)} %convert_element_type.99), channel_id=1, replica_groups=mesh['expert'=32,'dp'=4] {'expert'}, dimensions={0} | all-to-all | bytes 4608 | tf_op jit(solution)/shard_map/all_to_all | solution.py:56
  150.5 40.2 %reduce-scatter.8.cloned.1.call-done = f32[1,32,36,256]{3,2,1,0:T(8,128)} async-done(((f32[1,32,36,1024]{3,2,1,0:T(8,128)}), f32[1,32,36,256]{3,2,1,0:T(8,128)}) %reduce-scatter.8.cloned.1.call-update) | async-done | bytes 1179664 | tf_op jit(solution)/shard_map/reduce_scatter | solution.py:70
  190.7 57.6 %reduce-scatter.4.cloned.1.call-done = f32[1,32,36,256]{3,2,1,0:T(8,128)} async-done(((f32[1,32,36,1024]{3,2,1,0:T(8,128)}), f32[1,32,36,256]{3,2,1,0:T(8,128)}) %reduce-scatter.4.cloned.1.call-update) | async-done | bytes 1179664 | tf_op jit(solution)/shard_map/reduce_scatter | solution.py:72
  248.3 4.3 %multiply_reduce_fusion = (bf16[32,36]{1,0:T(8,128)(2,1)S(1)}, bf16[1,32,36,256]{3,2,1,0:T(8,128)(2,1)}, bf16[1,32,36,256]{3,2,1,0:T(8,128)(2,1)}, bf16[1,32,36,256]{3,2,1,0:T(8,128)(2,1)}) fusion(f32[1,32,36,256]{3,2,1,0:T(8,128)} %reduce-scatter.4.cloned.1.call-done, f32[1,32,36,256]{3,2,1,0:T(8,128)} %reduce-scatter.6.cloned.1.call-done, ...), kind=kLoop, calls=%fused_computation.34 | loop fusion | flops 5602176 | bytes 5315328 | tf_op jit(solution)/shard_map/reduce_sum | solution.py:77
  252.7 0.5 all-gather.4.cloned.1.call-update
  253.2 0.1 copy.66
  253.3 0.1 mul.87
  253.4 9.0 %all_gather.14 = bf16[1,32,36,4]{2,1,0,3:T(8,128)(2,1)S(1)} all-gather(bf16[1,32,36,1]{2,1,0,3:T(8,128)(2,1)S(1)} %bitcast.97), channel_id=1, replica_groups=mesh['expert'=32,'dp'=4] {'dp'}, dimensions={3}, use_global_device_ids=true | all-gather | bytes 11520 | tf_op jit(solution)/shard_map/all_gather | solution.py:82
  262.5 0.6 copy.68
  263.1 10.4 %all-to-all-start.4 = ((bf16[32,36,4]{1,2,0:T(4,128)(2,1)}), bf16[32,36,4]{1,2,0:T(4,128)(2,1)S(1)}, u32[]{:S(2)}, u32[]{:S(2)}) async-start(bf16[32,36,4]{1,2,0:T(4,128)(2,1)} %copy.68), calls=%async_computation.7 | async-start | bytes 65536 | tf_op jit(solution)/shard_map/all_to_all | solution.py:106
  273.5 0.0 all-gather.8.cloned.1.call-start
  273.5 0.1 copy.63
  273.7 0.4 all-gather.8.cloned.1.call-update
  274.1 6.7 %all-to-all-done.4 = bf16[32,36,4]{1,2,0:T(4,128)(2,1)S(1)} async-done(((bf16[32,36,4]{1,2,0:T(4,128)(2,1)}), bf16[32,36,4]{1,2,0:T(4,128)(2,1)S(1)}, u32[]{:S(2)}, u32[]{:S(2)}) %all-to-all-start.4) | async-done | bytes 9248 | tf_op jit(solution)/shard_map/all_to_all | solution.py:106
  280.7 0.1 all_to_all.39
  280.9 0.2 copy.70
  281.1 3.2 gather_fusion.1
  284.3 0.3 convert_reduce_fusion
  284.6 0.1 reshape.213
  284.7 0.7 copy.71
  285.4 5.1 %all-gather.6.cloned.1.call-done = bf16[1,32,36,1024]{3,2,1,0:T(8,128)(2,1)} async-done(((bf16[1,32,36,256]{3,2,1,0:T(8,128)(2,1)}), bf16[1,32,36,1024]{3,2,1,0:T(8,128)(2,1)}) %all-gather.6.cloned.1.call-update) | async-done | bytes 2359312 | tf_op jit(solution)/shard_map/all_gather | solution.py:81
  290.5 6.4 %fusion.5 = f32[32,36,1024]{2,1,0:T(8,128)} fusion(bf16[1,32,36,1024]{3,2,1,0:T(8,128)(2,1)} %all-gather.6.cloned.1.call-done, bf16[1,1024,1024]{2,1,0:T(8,128)(2,1)S(1)} %copy-done), kind=kOutput, calls=%fused_computation.13 | convolution fusion | flops 2415919104 | bytes 9175040 | tf_op jit(solution)/shard_map/escf,edf->secd/dot_general | solution.py:87
  296.9 35.6 %all-gather.4.cloned.1.call-done = bf16[1,32,36,1024]{3,2,1,0:T(8,128)(2,1)} async-done(((bf16[1,32,36,256]{3,2,1,0:T(8,128)(2,1)}), bf16[1,32,36,1024]{3,2,1,0:T(8,128)(2,1)}) %all-gather.4.cloned.1.call-update) | async-done | bytes 2359312 | tf_op jit(solution)/shard_map/all_gather | solution.py:80
  332.5 8.3 %add_convert_fusion = bf16[32,36,1024]{2,1,0:T(8,128)(2,1)} fusion(f32[32,36,1024]{2,1,0:T(8,128)} %fusion.5, bf16[1,1024,1024]{2,1,0:T(8,128)(2,1)} %param.11, bf16[1,32,36,1024]{3,2,1,0:T(8,128)(2,1)} %all-gather.4.cloned.1.call-done), kind=kOutput, calls=%fused_computation.2 | convolution fusion | flops 2418278400 | bytes 11534336 | tf_op jit(solution)/shard_map/escf,edf->secd/dot_general | solution.py:84
  340.8 8.5 %all-to-all-start.3 = ((bf16[32,36,1024]{2,1,0:T(8,128)(2,1)}), bf16[32,36,1024]{2,1,0:T(8,128)(2,1)}, u32[]{:S(2)}, u32[]{:S(2)}) async-start(bf16[32,36,1024]{2,1,0:T(8,128)(2,1)} %add_convert_fusion), calls=%async_computation.6 | async-start | bytes 5242880 | tf_op jit(solution)/shard_map/all_to_all | solution.py:105
  349.3 7.7 %fusion.12 = f32[1,1024,1024]{2,1,0:T(8,128)} fusion(bf16[32,36,1024]{2,1,0:T(8,128)(2,1)} %copy-done.2, bf16[1,32,36,1024]{3,2,1,0:T(8,128)(2,1)} %all-gather.4.cloned.1.call-done), kind=kOutput, calls=%fused_computation.23 | convolution fusion | flops 2415919104 | bytes 8912896 | tf_op jit(solution)/shard_map/secd,escf->edf/dot_general | solution.py:97
  356.9 4.4 %fusion.15 = f32[1,1024,1024]{2,1,0:T(8,128)} fusion(bf16[32,36,1024]{2,1,0:T(8,128)(2,1)S(1)} %copy-done.3, bf16[1,32,36,1024]{3,2,1,0:T(8,128)(2,1)S(1)} %copy-done.8), kind=kOutput, calls=%fused_computation.24 | convolution fusion | flops 2415919104 | bytes 8912896 | tf_op jit(solution)/shard_map/secd,escf->edf/dot_general | solution.py:100
  361.4 13.1 %all-gather.8.cloned.1.call-done = bf16[1,32,36,1024]{3,2,1,0:T(8,128)(2,1)} async-done(((bf16[1,32,36,256]{3,2,1,0:T(8,128)(2,1)}), bf16[1,32,36,1024]{3,2,1,0:T(8,128)(2,1)}) %all-gather.8.cloned.1.call-update) | async-done | bytes 2359312 | tf_op jit(solution)/shard_map/all_gather | solution.py:79
  374.5 7.5 %fusion.18 = f32[1,1024,1024]{2,1,0:T(8,128)} fusion(bf16[32,36,1024]{2,1,0:T(8,128)(2,1)} %copy-done.4, bf16[1,32,36,1024]{3,2,1,0:T(8,128)(2,1)} %all-gather.8.cloned.1.call-done, bf16[32,36]{1,0:T(8,128)(2,1)S(1)} %get-tuple-element.37), kind=kOutput, calls=%fused_computation.25 | convolution fusion | flops 2417098752 | bytes 8915200 | tf_op jit(solution)/shard_map/escf,secd->efd/dot_general | solution.py:94
  382.0 0.8 all-to-all-done.3
  382.9 4.1 %all_to_all.36 = bf16[1152,1024]{1,0:T(8,128)(2,1)} reshape(bf16[32,36,1024]{2,1,0:T(8,128)(2,1)} %all-to-all-done.3) | data formatting | bytes 4718592 | tf_op jit(solution)/shard_map/all_to_all | solution.py:105
  386.9 8.1 %gather_fusion = bf16[1024,1024]{1,0:T(8,128)(2,1)} fusion(bf16[1152,1024]{1,0:T(8,128)(2,1)} %all_to_all.36, s32[1024]{0:T(1024)S(1)} %broadcast_clamp_fusion), kind=kCustom, calls=%fused_computation | custom fusion | bytes 4198400 | tf_op jit(solution)/shard_map/jit(_take)/gather | solution.py:108
  395.1 3.4 fusion.23
  (34 shorter events, 0.4 us)
Async XLA Ops:
  7.2 67.0 %copy-start = (bf16[1,1024,1024]{2,1,0:T(8,128)(2,1)S(1)}, bf16[1,1024,1024]{2,1,0:T(8,128)(2,1)}, u32[]{:S(2)}) copy-start(bf16[1,1024,1024]{2,1,0:T(8,128)(2,1)} %param.12) | copy-start | bytes 6291460
  7.2 143.3 %reduce-scatter.6.cloned.1.call-start = ((), (), s32[]{:S(2)}) async-start(), calls=%async_computation.9 | async-start | bytes 6553600 | tf_op jit(solution)/shard_map/reduce_scatter | solution.py:71
  72.7 1.5 copy-start.2
  78.8 111.9 %reduce-scatter.8.cloned.1.call-start = ((), (), s32[]{:S(2)}) async-start(), calls=%async_computation.10 | async-start | bytes 6553600 | tf_op jit(solution)/shard_map/reduce_scatter | solution.py:70
  86.5 1.0 copy-start.5
  86.5 161.8 %reduce-scatter.4.cloned.1.call-start = ((), (), s32[]{:S(2)}) async-start(), calls=%async_computation.8 | async-start | bytes 6553600 | tf_op jit(solution)/shard_map/reduce_scatter | solution.py:72
  93.8 39.9 %copy-start.9 = (bf16[1,1024,1024]{2,1,0:T(8,128)(2,1)S(1)}, bf16[1,1024,1024]{2,1,0:T(8,128)(2,1)}, u32[]{:S(2)}) copy-start(bf16[1,1024,1024]{2,1,0:T(8,128)(2,1)} %param.13) | copy-start | bytes 6291460
  132.2 1.5 copy-start.4
  138.4 0.7 copy-start.7
  138.4 152.1 %all-gather.6.cloned.1.call-start = ((), (), s32[]{:S(2)}) async-start(), calls=%async_computation.12 | async-start | bytes 3276800 | tf_op jit(solution)/shard_map/all_gather | solution.py:81
  248.3 4.9 %copy-start.6 = (s32[128,8]{0,1:T(8,128)S(1)}, s32[128,8]{0,1:T(8,128)}, u32[]{:S(2)}) copy-start(s32[128,8]{0,1:T(8,128)} %param.10) | copy-start | bytes 12292
  252.6 79.9 %all-gather.4.cloned.1.call-start = ((), (), s32[]{:S(2)}) async-start(), calls=%async_computation.11 | async-start | bytes 3276800 | tf_op jit(solution)/shard_map/all_gather | solution.py:80
  263.1 17.6 %all-to-all-start.4 = ((bf16[32,36,4]{1,2,0:T(4,128)(2,1)}), bf16[32,36,4]{1,2,0:T(4,128)(2,1)S(1)}, u32[]{:S(2)}, u32[]{:S(2)}) async-start(bf16[32,36,4]{1,2,0:T(4,128)(2,1)} %copy.68), calls=%async_computation.7 | async-start | bytes 65536 | tf_op jit(solution)/shard_map/all_to_all | solution.py:106
  273.5 101.0 %all-gather.8.cloned.1.call-start = ((), (), s32[]{:S(2)}) async-start(), calls=%async_computation.13 | async-start | bytes 3276800 | tf_op jit(solution)/shard_map/all_gather | solution.py:79
  340.8 42.1 %all-to-all-start.3 = ((bf16[32,36,1024]{2,1,0:T(8,128)(2,1)}), bf16[32,36,1024]{2,1,0:T(8,128)(2,1)}, u32[]{:S(2)}, u32[]{:S(2)}) async-start(bf16[32,36,1024]{2,1,0:T(8,128)(2,1)} %add_convert_fusion), calls=%async_computation.6 | async-start | bytes 5242880 | tf_op jit(solution)/shard_map/all_to_all | solution.py:105
  349.3 7.7 %copy-start.3 = (bf16[32,36,1024]{2,1,0:T(8,128)(2,1)S(1)}, bf16[32,36,1024]{2,1,0:T(8,128)(2,1)}, u32[]{:S(2)}) copy-start(bf16[32,36,1024]{2,1,0:T(8,128)(2,1)} %copy-done.2) | copy-start | bytes 7077892
  349.3 7.7 %copy-start.8 = (bf16[1,32,36,1024]{3,2,1,0:T(8,128)(2,1)S(1)}, bf16[1,32,36,1024]{3,2,1,0:T(8,128)(2,1)}, u32[]{:S(2)}) copy-start(bf16[1,32,36,1024]{3,2,1,0:T(8,128)(2,1)} %all-gather.6.cloned.1.call-done) | copy-start | bytes 7077892
  386.9 11.5 %copy-start.1 = (bf16[1,1024,1024]{2,1,0:T(8,128)(2,1)S(1)}, bf16[1,1024,1024]{2,1,0:T(8,128)(2,1)}, u32[]{:S(2)}) copy-start(bf16[1,1024,1024]{2,1,0:T(8,128)(2,1)} %param.12) | copy-start | bytes 6291460
Sparse Core Ops, SparseCore 0:
  78.9 54.0 reduce-scatter.5
  135.5 55.1 reduce-scatter.7
  193.1 55.1 reduce-scatter.3
  252.7 37.7 all-gather.5
  292.6 39.8 all-gather.3
  334.6 39.8 all-gather.7
where the time goes:
time: 408 us; the launch traced here: 405 us
  waiting for transfers between devices  160 us (39%)
  blocking collectives  101 us (25%)
  matrix products  56.6 us (14%)
  local copies, waits for them, and re-layouts  32.1 us (8%)
  other arithmetic  22.7 us (6%)
  starting transfers between devices  19.1 us (5%)
  between operations  14.3 us (4%)
    reduce_scatter x1, waiting for transfers between devices, shards(): lax.psum_scatter(back_part, 'dp', scatter_dimension=3, tiled=True)  57.6 us
    all_to_all x1, blocking collectives, shards(): lax.all_to_all(x_send, 'expert', split_axis=0, concat_axis=0, tiled=True)  42.6 us
    reduce_scatter x1, waiting for transfers between devices, shards(): lax.psum_scatter(gate_part, 'dp', scatter_dimension=3, tiled=True)  40.2 us
    all_to_all x1, blocking collectives, shards(): lax.all_to_all(dy_send, 'expert', split_axis=0, concat_axis=0, tiled=True)  38.4 us
    all_gather x1, waiting for transfers between devices, shards(): lax.all_gather(grad_gate_pre, 'dp', axis=3, tiled=True)  35.6 us
    all_gather x1, waiting for transfers between devices, shards(): lax.all_gather(hidden, 'dp', axis=3, tiled=True)  13.1 us
    all_to_all x1, blocking collectives, shards(): lax.all_to_all(g_send, 'expert', split_axis=0, concat_axis=0, tiled=True)  10.6 us
    all_to_all x1, starting transfers between devices, shards(): lax.all_to_all(block_send, 'expert', split_axis=0, concat_axis=0, tiled=T...  10.4 us
  transfers between devices with their start and end apart: 8, of which 7 were waited for; matrix products, arithmetic and copies ran while one was open for 14% of the time, Pallas kernels for 0%

commit v1 on v0

v1 whole, which is shorter than its diff:
```python
import jax
import jax.numpy as jnp
from jax import lax
from jax.sharding import PartitionSpec as P

TOP = 8
EXPERTS = 32
CAP = 36


def dot32(spec, a, b):
    return jnp.einsum(spec, a, b, preferred_element_type=jnp.float32)


def hidden_units(gate_pre, up_pre, back_hidden, g_rows):
    sigmoid_gate = jax.nn.sigmoid(gate_pre)
    swish_gate = gate_pre * sigmoid_gate
    hidden = (swish_gate * up_pre).astype(jnp.bfloat16)
    product = back_hidden * hidden.astype(jnp.float32)
    grad_hidden = g_rows * back_hidden
    derivative = sigmoid_gate * (1.0 + gate_pre * (1.0 - sigmoid_gate))
    grad_gate_pre = (grad_hidden * up_pre * derivative).astype(jnp.bfloat16)
    grad_up_pre = (grad_hidden * swish_gate).astype(jnp.bfloat16)
    return (hidden, grad_gate_pre, grad_up_pre, product)


def shards(tokens, cotangent, gate_probs, expert_ids, gate_weight, up_weight, down_weight):
    me = lax.axis_index("expert")
    groups = lax.axis_size("expert")
    count, width = tokens.shape
    wg, wu, wd = gate_weight[0], up_weight[0], down_weight[0]
    columns = jnp.arange(128, dtype=jnp.int32)
    chosen = expert_ids[:, :, None] == columns[None, None, :]
    routed = jnp.sum(jnp.where(chosen, gate_probs[:, :, None].astype(jnp.float32), 0.0), axis=1)
    routed = routed.astype(jnp.bfloat16)
    everything = lax.all_gather(
        jnp.concatenate([tokens, cotangent, routed], axis=1), "expert", axis=0, tiled=False
    )
    x_all, dy_all = everything[:, :, :width], everything[:, :, width : 2 * width]
    mine = jnp.sum(
        jnp.where(columns[None, None, :] == me, everything[:, :, 2 * width :], 0), axis=2
    )
    before = (jnp.arange(count)[:, None] < jnp.arange(count)[None, :]).astype(jnp.bfloat16)
    member = (mine > 0).astype(jnp.bfloat16)
    rank = dot32("gt,tu->gu", member, before)
    slots = jnp.arange(CAP, dtype=jnp.float32)
    pick = (rank[:, None, :] == slots[None, :, None]) & (mine[:, None, :] > 0)
    g_rows = jnp.sum(jnp.where(pick, mine[:, None, :].astype(jnp.float32), 0.0), axis=2)
    pick = pick.astype(jnp.bfloat16)
    rows = groups * CAP
    x_rows = dot32("gst,gtd->gsd", pick, x_all).astype(jnp.bfloat16).reshape(rows, width)
    dy_rows = dot32("gst,gtd->gsd", pick, dy_all).astype(jnp.bfloat16).reshape(rows, width)
    g_rows = g_rows.reshape(rows, 1)
    parts = (
        dot32("rd,df->rf", x_rows, wg).astype(jnp.bfloat16),
        dot32("rd,df->rf", x_rows, wu).astype(jnp.bfloat16),
        dot32("rd,fd->rf", dy_rows, wd).astype(jnp.bfloat16),
    )
    gate_pre, up_pre, back_hidden = (
        lax.psum_scatter(part, "dp", scatter_dimension=1, tiled=True).astype(jnp.float32)
        for part in parts
    )
    hidden, grad_gate_pre, grad_up_pre, product = hidden_units(
        gate_pre, up_pre, back_hidden, g_rows
    )
    block_sum = jnp.sum(product, axis=1, keepdims=True).astype(jnp.bfloat16)
    hidden, grad_gate_pre, grad_up_pre, gate_blocks = (
        lax.all_gather(part, "dp", axis=1, tiled=True)
        for part in (hidden, grad_gate_pre, grad_up_pre, block_sum)
    )
    input_part = dot32("rf,df->rd", grad_gate_pre, wg) + dot32("rf,df->rd", grad_up_pre, wu)
    input_part = input_part.astype(jnp.bfloat16)
    scaled_dy = (dy_rows.astype(jnp.float32) * g_rows).astype(jnp.bfloat16)
    grad_down = dot32("rf,rd->fd", hidden, scaled_dy)
    grad_gate = dot32("rd,rf->df", x_rows, grad_gate_pre)
    grad_up = dot32("rd,rf->df", x_rows, grad_up_pre)
    input_table = lax.all_to_all(
        input_part.reshape(groups, CAP, width), "expert", split_axis=0, concat_axis=0
    )
    gate_table = lax.all_to_all(
        gate_blocks.reshape(groups, CAP, -1), "expert", split_axis=0, concat_axis=0
    )
    gate_table = jnp.sum(gate_table.astype(jnp.float32), axis=2)
    local = routed[:, :EXPERTS]
    local_rank = dot32("tu,te->ue", before, (local > 0).astype(jnp.bfloat16))
    place = (local_rank[:, :, None] == slots[None, None, :]) & (local[:, :, None] > 0)
    by_expert = jnp.sum(jnp.where(place, gate_table[None], 0.0), axis=2)
    grad_gates = jnp.sum(jnp.where(chosen[:, :, :EXPERTS], by_expert[:, None, :], 0.0), axis=2)
    place = place.astype(jnp.bfloat16).reshape(count, rows)
    grad_tokens = dot32("tr,rd->td", place, input_table.reshape(rows, width)).astype(jnp.bfloat16)
    return (grad_tokens, grad_gates, grad_gate[None], grad_up[None], grad_down[None])


def solution(mesh):
    placed = (
        P("expert", "dp"),
        P("expert", "dp"),
        P("expert", None),
        P("expert", None),
        P("expert", "dp", None),
        P("expert", "dp", None),
        P("expert", None, "dp"),
    )
    return jax.shard_map(
        shards,
        mesh=mesh,
        in_specs=placed,
        out_specs=(
            P("expert", "dp"),
            P("expert", None),
            P("expert", "dp", None),
            P("expert", "dp", None),
            P("expert", None, "dp"),
        ),
        check_vma=False,
    )
```

time: 408 us -> 353 us (0.87)
  blocking collectives: 101 us -> 9.05 us
  waiting for transfers between devices: 160 us -> 218 us
  local copies, waits for them, and re-layouts: 32.1 us -> 13.4 us
  other arithmetic: 22.7 us -> 9.98 us
  matrix products: 56.6 us -> 67.1 us
    all_to_all x3 -> x0, blocking collectives: 91.6 us -> none  [the longest x1 42.6 us: shards(): lax.all_to_all(x_send, 'expert', split_axis=0, concat_axis=0, tiled=True)]
    all_gather x3 -> x4, waiting for transfers between devices: 53.7 us -> 132 us  [the longest x1 78.5 us: shards(): lax.all_gather(jnp.concatenate([tokens, cotangent, routed], axis=1), 'exp...]
    reduce_scatter x3, waiting for transfers between devices: 97.8 us -> 77.2 us  [shards(): lax.psum_scatter(part, 'dp', scatter_dimension=1, tiled=True)]
    all_to_all x7 -> x0, local copies, waits for them, and re-layouts: 13.2 us -> none  [the longest x1 4.08 us: shards(): lax.all_to_all(input_part, 'expert', split_axis=0, concat_axis=0, tiled=T...]
    reshape x2 -> x5, local copies, waits for them, and re-layouts: 0.18 us -> 13 us  [the longest x1 4.1 us: shards(): dot32('gst,gtd->gsd', pick, x_all).astype(jnp.bfloat16).reshape(rows, width)]
    gather x2 -> x0, local copies, waits for them, and re-layouts: 11.3 us -> none  [the longest x1 8.13 us: shards(): picked = jnp.take(input_table, target, axis=0).astype(jnp.float32)]
    dot_general x10 -> x13, matrix products: 56.6 us -> 67.1 us  [dot32(): return jnp.einsum(spec, a, b, preferred_element_type=jnp.float32)]
    another operation x2 -> x0, other arithmetic: 9.04 us -> none
  transfers between devices with their start and end apart: 8 -> 9, of which waited for: 7 -> 8; matrix products, arithmetic and copies ran while one was open for 14% -> 18% of each run, Pallas kernels for 0% -> 0%
where the time goes in v1:
time: 353 us; the launch traced here: 351 us
  waiting for transfers between devices  218 us (62%)
  matrix products  67.1 us (19%)
  starting transfers between devices  19.1 us (5%)
  between operations  14.3 us (4%)
  local copies, waits for them, and re-layouts  13.4 us (4%)
  other arithmetic  9.98 us (3%)
  blocking collectives  9.05 us (3%)
    all_gather x1, waiting for transfers between devices, shards(): lax.all_gather(jnp.concatenate([tokens, cotangent, routed], axis=1), 'exp...  78.5 us
    reduce_scatter x3, waiting for transfers between devices, shards(): lax.psum_scatter(part, 'dp', scatter_dimension=1, tiled=True)  77.2 us
    dot_general x13, matrix products, dot32(): return jnp.einsum(spec, a, b, preferred_element_type=jnp.float32)  67.1 us
    all_gather x3, waiting for transfers between devices, shards(): lax.all_gather(part, 'dp', axis=1, tiled=True)  53.8 us
    all_to_all x1, starting transfers between devices, shards(): lax.all_to_all(gate_blocks.reshape(groups, CAP, -1), 'expert', split_axis...  10.4 us
    all_gather x1, blocking collectives, shards(): lax.all_gather(part, 'dp', axis=1, tiled=True)  9.05 us
    all_to_all x1, starting transfers between devices, shards(): lax.all_to_all(input_part.reshape(groups, CAP, width), 'expert', split_ax...  8.44 us
  transfers between devices with their start and end apart: 9, of which 8 were waited for; matrix products, arithmetic and copies ran while one was open for 18% of the time, Pallas kernels for 0%

profile of v1, /device:TPU:1, one launch (start us, length us, event | category | flops | bytes accessed | tf_op | source)
XLA Modules:
  0.0 350.5 jit_solution(10511176142341472785)
XLA Ops:
  7.2 0.0 copy-start
  7.2 0.0 all-gather.13.cloned.1.call-start
  7.2 0.8 convert_element_type.89
  8.1 0.7 select_reduce_fusion.2
  8.8 0.1 copy.27
  8.9 1.9 pad_maximum_fusion
  10.8 0.0 all-gather.13.cloned.1.call-update
  10.8 0.0 reduce-scatter.4.cloned.1.call-start
  10.9 78.5 %all-gather.13.cloned.1.call-done = bf16[4096,2176]{1,0:T(8,128)(2,1)} async-done(((bf16[128,2176]{1,0:T(8,128)(2,1)}), bf16[4096,2176]{1,0:T(8,128)(2,1)}) %all-gather.13.cloned.1.call-update) | async-done | bytes 17825808 | tf_op jit(solution)/shard_map/all_gather | solution.py:36
  89.4 1.6 fusion.31
  91.0 0.1 fusion.43
  91.1 6.1 %fusion.13 = bf16[32,36,1024]{2,1,0:T(8,128)(2,1)} fusion(bf16[32,128,2176]{2,1,0:T(8,128)(2,1)} %bitcast.45, f32[32,128]{1,0:T(8,128)S(1)} %fusion.43, pred[32,128]{1,0:T(8,128)(4,1)S(1)} %broadcast_compare_fusion), kind=kOutput, calls=%fused_computation.20 | convolution fusion | flops 303464448 | bytes 10768384 | tf_op jit(solution)/shard_map/gst,gtd->gsd/dot_general | solution.py:12
  97.2 4.1 %reshape.57 = bf16[1152,1024]{1,0:T(8,128)(2,1)} reshape(bf16[32,36,1024]{2,1,0:T(8,128)(2,1)} %fusion.13) | data formatting | bytes 4718592 | tf_op jit(solution)/shard_map/reshape | solution.py:52
  101.3 6.4 %convolution_convert_fusion.2 = bf16[1152,1024]{1,0:T(8,128)(2,1)} fusion(bf16[1152,1024]{1,0:T(8,128)(2,1)} %reshape.57, bf16[1,1024,1024]{2,1,0:T(8,128)(2,1)} %param.13), kind=kOutput, calls=%fused_computation.8 | convolution fusion | flops 2417098752 | bytes 6815744 | tf_op jit(solution)/shard_map/rd,fd->rf/dot_general | solution.py:12
  107.7 0.0 reduce-scatter.4.cloned.1.call-update
  107.7 0.0 reduce-scatter.8.cloned.1.call-start
  107.8 6.1 %fusion.16 = bf16[32,36,1024]{2,1,0:T(8,128)(2,1)} fusion(bf16[32,128,2176]{2,1,0:T(8,128)(2,1)} %bitcast.46, f32[32,128]{1,0:T(8,128)S(1)} %fusion.43, pred[32,128]{1,0:T(8,128)(4,1)S(1)} %broadcast_compare_fusion), kind=kOutput, calls=%fused_computation.21 | convolution fusion | flops 303464448 | bytes 10768384 | tf_op jit(solution)/shard_map/gst,gtd->gsd/dot_general | solution.py:12
  113.9 4.1 %reshape.58 = bf16[1152,1024]{1,0:T(8,128)(2,1)} reshape(bf16[32,36,1024]{2,1,0:T(8,128)(2,1)} %fusion.16) | data formatting | bytes 4718592 | tf_op jit(solution)/shard_map/reshape | solution.py:51
  118.0 0.0 copy-done
  118.0 5.6 %convolution_convert_fusion = bf16[1152,1024]{1,0:T(8,128)(2,1)} fusion(bf16[1152,1024]{1,0:T(8,128)(2,1)} %reshape.58, bf16[1,1024,1024]{2,1,0:T(8,128)(2,1)S(1)} %copy-done), kind=kOutput, calls=%fused_computation.6 | convolution fusion | flops 2417098752 | bytes 6815744 | tf_op jit(solution)/shard_map/rd,df->rf/dot_general | solution.py:12
  123.6 0.0 reduce-scatter.8.cloned.1.call-update
  123.6 0.0 reduce-scatter.6.cloned.1.call-start
  123.7 6.4 %convolution_convert_fusion.1 = bf16[1152,1024]{1,0:T(8,128)(2,1)} fusion(bf16[1152,1024]{1,0:T(8,128)(2,1)} %reshape.58, bf16[1,1024,1024]{2,1,0:T(8,128)(2,1)} %param.12), kind=kOutput, calls=%fused_computation.7 | convolution fusion | flops 2417098752 | bytes 6815744 | tf_op jit(solution)/shard_map/rd,df->rf/dot_general | solution.py:12
  130.0 0.0 reduce-scatter.6.cloned.1.call-update
  130.1 0.0 all-gather.7.cloned.1.call-start
  130.1 0.3 select_reduce_fusion.1
  130.4 0.1 mul.42
  130.5 0.0 copy-start.3
  130.5 8.6 %reduce-scatter.4.cloned.1.call-done = bf16[1152,256]{1,0:T(8,128)(2,1)} async-done(((bf16[1152,1024]{1,0:T(8,128)(2,1)}), bf16[1152,256]{1,0:T(8,128)(2,1)}) %reduce-scatter.4.cloned.1.call-update) | async-done | bytes 589840 | tf_op jit(solution)/shard_map/reduce_scatter | solution.py:60
  139.1 34.1 %reduce-scatter.8.cloned.1.call-done = bf16[1152,256]{1,0:T(8,128)(2,1)} async-done(((bf16[1152,1024]{1,0:T(8,128)(2,1)}), bf16[1152,256]{1,0:T(8,128)(2,1)}) %reduce-scatter.8.cloned.1.call-update) | async-done | bytes 589840 | tf_op jit(solution)/shard_map/reduce_scatter | solution.py:60
  173.2 34.5 %reduce-scatter.6.cloned.1.call-done = bf16[1152,256]{1,0:T(8,128)(2,1)} async-done(((bf16[1152,1024]{1,0:T(8,128)(2,1)}), bf16[1152,256]{1,0:T(8,128)(2,1)}) %reduce-scatter.6.cloned.1.call-update) | async-done | bytes 589840 | tf_op jit(solution)/shard_map/reduce_scatter | solution.py:60
  207.7 3.5 %fusion.22 = (bf16[1152]{0:T(1024)(128)(2,1)S(1)}, bf16[1152,256]{1,0:T(8,128)(2,1)}, bf16[1152,256]{1,0:T(8,128)(2,1)}, bf16[1152,256]{1,0:T(8,128)(2,1)}) fusion(bf16[1152,256]{1,0:T(8,128)(2,1)} %reduce-scatter.4.cloned.1.call-done, bf16[1152,256]{1,0:T(8,128)(2,1)} %reduce-scatter.6.cloned.1.call-done, ...), kind=kLoop, calls=%fused_computation.33 | loop fusion | flops 6486912 | bytes 3545856 | tf_op jit(solution)/shard_map/reduce_sum | solution.py:66
  211.2 0.0 all-gather.7.cloned.1.call-update
  211.2 0.0 all-gather.9.cloned.1.call-start
  211.3 0.5 all-gather.9.cloned.1.call-update
  211.8 0.0 all-gather.11.cloned.1.call-start
  211.9 0.7 all-gather.11.cloned.1.call-update
  212.6 0.0 copy-done.3
  212.6 0.1 iota_compare_fusion.2
  212.7 9.1 %all-gather.1 = bf16[4,1,1152]{2,1,0:T(2,128)(2,1)S(1)} all-gather(bf16[1,1,1152]{2,1,0:T(2,128)(2,1)S(1)} %reshape.62), channel_id=1, replica_groups=mesh['expert'=32,'dp'=4] {'dp'}, dimensions={0}, use_global_device_ids=true | all-gather | bytes 11520 | tf_op jit(solution)/shard_map/all_gather | solution.py:68
  221.7 0.1 reshape.60
  221.9 0.6 copy.25
  222.5 10.4 %all-to-all-start.1 = ((bf16[32,36,4]{1,2,0:T(4,128)(2,1)}), bf16[32,36,4]{1,2,0:T(4,128)(2,1)S(1)}, u32[]{:S(2)}, u32[]{:S(2)}) async-start(bf16[32,36,4]{1,2,0:T(4,128)(2,1)} %copy.25), calls=%async_computation.4 | async-start | bytes 65536 | tf_op jit(solution)/shard_map/all_to_all | solution.py:80
  232.9 14.0 %all-gather.7.cloned.1.call-done = bf16[1152,1024]{1,0:T(8,128)(2,1)} async-done(((bf16[1152,256]{1,0:T(8,128)(2,1)}), bf16[1152,1024]{1,0:T(8,128)(2,1)}) %all-gather.7.cloned.1.call-update) | async-done | bytes 2359312 | tf_op jit(solution)/shard_map/all_gather | solution.py:68
  246.9 6.0 %fusion.7 = f32[1152,1024]{1,0:T(8,128)} fusion(bf16[1152,1024]{1,0:T(8,128)(2,1)} %all-gather.7.cloned.1.call-done, bf16[1,1024,1024]{2,1,0:T(8,128)(2,1)S(1)} %copy-done), kind=kOutput, calls=%fused_computation.14 | convolution fusion | flops 2415919104 | bytes 9175040 | tf_op jit(solution)/shard_map/rf,df->rd/dot_general | solution.py:12
  252.9 33.8 %all-gather.9.cloned.1.call-done = bf16[1152,1024]{1,0:T(8,128)(2,1)} async-done(((bf16[1152,256]{1,0:T(8,128)(2,1)}), bf16[1152,1024]{1,0:T(8,128)(2,1)}) %all-gather.9.cloned.1.call-update) | async-done | bytes 2359312 | tf_op jit(solution)/shard_map/all_gather | solution.py:68
  286.8 7.7 %add_convert_fusion = bf16[1152,1024]{1,0:T(8,128)(2,1)} fusion(f32[1152,1024]{1,0:T(8,128)} %fusion.7, bf16[1152,1024]{1,0:T(8,128)(2,1)} %all-gather.9.cloned.1.call-done, bf16[1,1024,1024]{2,1,0:T(8,128)(2,1)} %param.12), kind=kOutput, calls=%fused_computation.5 | convolution fusion | flops 2418278400 | bytes 11534336 | tf_op jit(solution)/shard_map/rf,df->rd/dot_general | solution.py:12
  294.5 4.1 %reshape.59 = bf16[32,36,1024]{2,1,0:T(8,128)(2,1)} reshape(bf16[1152,1024]{1,0:T(8,128)(2,1)} %add_convert_fusion) | data formatting | bytes 4718592 | tf_op jit(solution)/shard_map/reshape | solution.py:78
  298.6 0.0 all-to-all-done.1
  298.6 8.4 %all-to-all-start = ((bf16[32,36,1024]{2,1,0:T(8,128)(2,1)}), bf16[32,36,1024]{2,1,0:T(8,128)(2,1)}, u32[]{:S(2)}, u32[]{:S(2)}) async-start(bf16[32,36,1024]{2,1,0:T(8,128)(2,1)} %reshape.59), calls=%async_computation.3 | async-start | bytes 5242880 | tf_op jit(solution)/shard_map/all_to_all | solution.py:77
  307.0 0.2 fusion.44
  307.2 0.1 copy.24
  307.3 0.1 convert_reduce_fusion
  307.4 0.3 select_reduce_fusion
  307.7 0.6 select_reduce_fusion.3
  308.3 7.5 %convolution_bitcast_fusion = f32[1,1024,1024]{2,1,0:T(8,128)} fusion(bf16[1152,1024]{1,0:T(8,128)(2,1)} %reshape.58, bf16[1152,1024]{1,0:T(8,128)(2,1)} %all-gather.9.cloned.1.call-done), kind=kOutput, calls=%fused_computation.12 | convolution fusion | flops 2415919104 | bytes 8912896 | tf_op jit(solution)/shard_map/rd,rf->df/dot_general | solution.py:12
  315.8 0.0 copy-done.2
  315.8 0.0 copy-done.4
  315.8 4.4 %convolution_bitcast_fusion.1 = f32[1,1024,1024]{2,1,0:T(8,128)} fusion(bf16[1152,1024]{1,0:T(8,128)(2,1)S(1)} %copy-done.2, bf16[1152,1024]{1,0:T(8,128)(2,1)S(1)} %copy-done.4), kind=kOutput, calls=%fused_computation.13 | convolution fusion | flops 2415919104 | bytes 8912896 | tf_op jit(solution)/shard_map/rd,rf->df/dot_general | solution.py:12
  320.2 5.9 %all-gather.11.cloned.1.call-done = bf16[1152,1024]{1,0:T(8,128)(2,1)} async-done(((bf16[1152,256]{1,0:T(8,128)(2,1)}), bf16[1152,1024]{1,0:T(8,128)(2,1)}) %all-gather.11.cloned.1.call-update) | async-done | bytes 2359312 | tf_op jit(solution)/shard_map/all_gather | solution.py:68
  326.2 7.6 %fusion.6 = f32[1,1024,1024]{2,1,0:T(8,128)} fusion(bf16[1152,1024]{1,0:T(8,128)(2,1)} %all-gather.11.cloned.1.call-done, bf16[1152,1024]{1,0:T(8,128)(2,1)} %reshape.57, f32[1152]{0:T(1024)S(1)} %mul.42), kind=kOutput, calls=%fused_computation.11 | convolution fusion | flops 2419458048 | bytes 8917504 | tf_op jit(solution)/shard_map/rf,rd->fd/dot_general | solution.py:12
  333.7 6.9 %all-to-all-done = bf16[32,36,1024]{2,1,0:T(8,128)(2,1)} async-done(((bf16[32,36,1024]{2,1,0:T(8,128)(2,1)}), bf16[32,36,1024]{2,1,0:T(8,128)(2,1)}, u32[]{:S(2)}, u32[]{:S(2)}) %all-to-all-start) | async-done | bytes 2359328 | tf_op jit(solution)/shard_map/all_to_all | solution.py:77
  340.6 3.0 fusion.20
  343.7 0.0 copy-done.1
  (9 shorter events, 0.0 us)
Async XLA Ops:
  7.2 110.8 %copy-start = (bf16[1,1024,1024]{2,1,0:T(8,128)(2,1)S(1)}, bf16[1,1024,1024]{2,1,0:T(8,128)(2,1)}, u32[]{:S(2)}) copy-start(bf16[1,1024,1024]{2,1,0:T(8,128)(2,1)} %param.11) | copy-start | bytes 6291460
  7.2 82.2 %all-gather.13.cloned.1.call-start = ((), (), s32[]{:S(2)}) async-start(), calls=%async_computation.11 | async-start | bytes 18382848 | tf_op jit(solution)/shard_map/all_gather | solution.py:36
  10.8 128.3 %reduce-scatter.4.cloned.1.call-start = ((), (), s32[]{:S(2)}) async-start(), calls=%async_computation.5 | async-start | bytes 2949120 | tf_op jit(solution)/shard_map/reduce_scatter | solution.py:60
  107.7 65.4 %reduce-scatter.8.cloned.1.call-start = ((), (), s32[]{:S(2)}) async-start(), calls=%async_computation.7 | async-start | bytes 2949120 | tf_op jit(solution)/shard_map/reduce_scatter | solution.py:60
  123.6 84.1 %reduce-scatter.6.cloned.1.call-start = ((), (), s32[]{:S(2)}) async-start(), calls=%async_computation.6 | async-start | bytes 2949120 | tf_op jit(solution)/shard_map/reduce_scatter | solution.py:60
  130.1 116.9 %all-gather.7.cloned.1.call-start = ((), (), s32[]{:S(2)}) async-start(), calls=%async_computation.8 | async-start | bytes 2949120 | tf_op jit(solution)/shard_map/all_gather | solution.py:68
  130.5 82.1 %copy-start.3 = (s32[128,8]{0,1:T(8,128)S(1)}, s32[128,8]{0,1:T(8,128)}, u32[]{:S(2)}) copy-start(s32[128,8]{0,1:T(8,128)} %param.10) | copy-start | bytes 12292
  211.2 75.5 %all-gather.9.cloned.1.call-start = ((), (), s32[]{:S(2)}) async-start(), calls=%async_computation.9 | async-start | bytes 2949120 | tf_op jit(solution)/shard_map/all_gather | solution.py:68
  211.8 114.4 %all-gather.11.cloned.1.call-start = ((), (), s32[]{:S(2)}) async-start(), calls=%async_computation.10 | async-start | bytes 2949120 | tf_op jit(solution)/shard_map/all_gather | solution.py:68
  222.5 76.1 %all-to-all-start.1 = ((bf16[32,36,4]{1,2,0:T(4,128)(2,1)}), bf16[32,36,4]{1,2,0:T(4,128)(2,1)S(1)}, u32[]{:S(2)}, u32[]{:S(2)}) async-start(bf16[32,36,4]{1,2,0:T(4,128)(2,1)} %copy.25), calls=%async_computation.4 | async-start | bytes 65536 | tf_op jit(solution)/shard_map/all_to_all | solution.py:80
  298.6 42.1 %all-to-all-start = ((bf16[32,36,1024]{2,1,0:T(8,128)(2,1)}), bf16[32,36,1024]{2,1,0:T(8,128)(2,1)}, u32[]{:S(2)}, u32[]{:S(2)}) async-start(bf16[32,36,1024]{2,1,0:T(8,128)(2,1)} %reshape.59), calls=%async_computation.3 | async-start | bytes 5242880 | tf_op jit(solution)/shard_map/all_to_all | solution.py:77
  308.3 7.5 %copy-start.2 = (bf16[1152,1024]{1,0:T(8,128)(2,1)S(1)}, bf16[1152,1024]{1,0:T(8,128)(2,1)}, u32[]{:S(2)}) copy-start(bf16[1152,1024]{1,0:T(8,128)(2,1)} %reshape.58) | copy-start | bytes 7077892
  308.3 7.5 %copy-start.4 = (bf16[1152,1024]{1,0:T(8,128)(2,1)S(1)}, bf16[1152,1024]{1,0:T(8,128)(2,1)}, u32[]{:S(2)}) copy-start(bf16[1152,1024]{1,0:T(8,128)(2,1)} %all-gather.7.cloned.1.call-done) | copy-start | bytes 7077892
  326.2 17.5 %copy-start.1 = (bf16[1,1024,1024]{2,1,0:T(8,128)(2,1)S(1)}, bf16[1,1024,1024]{2,1,0:T(8,128)(2,1)}, u32[]{:S(2)}) copy-start(bf16[1,1024,1024]{2,1,0:T(8,128)(2,1)} %param.11) | copy-start | bytes 6291460
Sparse Core Ops, SparseCore 0:
  10.9 78.4 all-gather.12
  107.8 31.1 reduce-scatter.3
  141.5 31.6 reduce-scatter.7
  176.0 31.6 reduce-scatter.5
  211.3 35.5 all-gather.6
  249.0 37.7 all-gather.8
  288.4 37.7 all-gather.10

commit v2 on v1

v2 whole, which is shorter than its diff:
```python
import functools

import jax
import jax.numpy as jnp
from jax import lax
from jax.experimental import pallas as pl
from jax.experimental.pallas import tpu as pltpu
from jax.sharding import PartitionSpec as P

EXPERTS = 32
CAP = 36
PAD = 40
HALF = 4 * CAP
ORDER = (0, 1, 3, 2)
BF = jnp.bfloat16
F32 = jnp.float32
MESH = pl.DeviceIdType.MESH
NT = (((1,), (1,)), ((), ()))
TN = (((0,), (0,)), ((), ()))


def dot32(spec, a, b):
    return jnp.einsum(spec, a, b, preferred_element_type=F32)


def mm(a, b):
    return jnp.dot(a, b, preferred_element_type=F32)


def mm_nt(a, b):
    return lax.dot_general(a, b, NT, preferred_element_type=F32)


def mm_tn(a, b):
    return lax.dot_general(a, b, TN, preferred_element_type=F32)


def landed(ref, sem):
    pltpu.make_async_copy(ref, ref, sem).wait()


def layer_kernel(
    tok_in, cot_in, routed_in, wg_in, wu_in, wd_in,
    xr_out, sdy_out, act_out, ret_out,
    tok, wg, wu, wd, routed, pick, g_rows, xr, sdy, dyr, part, r1, r2, act, prod, gates, inp, ret,
    own_sem, tok_s, tok_r, routed_s, routed_r, r1_s, r1_r, r2_s, r2_r, ag_s, ag_r,
    gates_s, gates_r, ret_s, ret_r, out_s,
):
    me = lax.axis_index("expert")
    z = lax.axis_index("dp")
    core = lax.rem(me, 2)
    chip_x = lax.rem(me // 2, 4)
    chip_y = me // 8
    a = chip_x * (1 - core) + chip_y * core
    b = chip_y * (1 - core) + chip_x * core

    def holder(side, da, db):
        kind = core if side == 0 else 1 - core
        first, second = (a, b) if side == 0 else (b, a)
        first, second = lax.rem(first + da, 4), lax.rem(second + db, 4)
        return ((1 - kind) * (second * 4 + first) + kind * (first * 4 + second)) * 2 + kind

    def plane(index):
        return {"expert": index}

    def column(step):
        return {"dp": lax.rem(z + step, 4)}

    partner = plane(me + 1 - 2 * core)
    sent = []

    def send(src, dst, ssem, rsem, device):
        copy = pltpu.make_async_remote_copy(
            src_ref=src, dst_ref=dst, send_sem=ssem, recv_sem=rsem,
            device_id=device, device_id_type=MESH,
        )
        copy.start()
        return copy

    loads = [
        pltpu.make_async_copy(tok_in, tok.at[0, 0, 0, 0], own_sem.at[0]),
        pltpu.make_async_copy(cot_in, tok.at[0, 0, 0, 1], own_sem.at[1]),
        pltpu.make_async_copy(routed_in.at[me], routed.at[me], own_sem.at[2]),
    ]
    weights = []
    for j in range(4):
        cols = pl.ds(j * 256, 256)
        weights.append(pltpu.make_async_copy(wg_in.at[:, cols], wg.at[j], own_sem.at[3 + j]))
        weights.append(pltpu.make_async_copy(wu_in.at[:, cols], wu.at[j], own_sem.at[7 + j]))
        weights.append(pltpu.make_async_copy(wd_in.at[cols], wd.at[j], own_sem.at[11 + j]))
    for copy in loads + weights:
        copy.start()

    barrier = pltpu.get_barrier_semaphore()

    def greet(d, carry):
        pl.semaphore_signal(
            barrier, inc=1, device_id=plane(lax.rem(me + d, 32)), device_id_type=MESH
        )
        return carry

    lax.fori_loop(1, 32, greet, 0)
    for step in (1, 2, 3):
        pl.semaphore_signal(barrier, inc=1, device_id=column(step), device_id_type=MESH)
    pl.semaphore_wait(barrier, 34)

    n_tok = [0]

    def send_tok(src, dst_index, device):
        sem = tok_s.at[n_tok[0]]
        n_tok[0] += 1
        sent.append(send(src, tok.at[dst_index], sem, tok_r.at[dst_index], device))

    def wait_tok(*index):
        landed(tok.at[index], tok_r.at[index])

    def cross(db, da):
        for arr in (0, 1):
            send_tok(tok.at[0, db, da, arr], (1, db, da, arr), partner)

    def second_axis(da):
        for arr in (0, 1):
            send_tok(tok.at[0, 0, da, arr], (0, 3, da, arr), plane(holder(0, da * 0, 1)))
            send_tok(tok.at[0, 0, da, 1 - arr], (0, 1, da, 1 - arr), plane(holder(0, 0, 3)))

    own = (tok_in, cot_in)
    for arr in (0, 1):
        send_tok(own[arr], (0, 0, 3, arr), plane(holder(0, 1, 0)))
        send_tok(own[1 - arr], (0, 0, 1, 1 - arr), plane(holder(0, 3, 0)))
    for arr in (0, 1):
        send_tok(own[arr], (1, 0, 0, arr), partner)

    def send_routed(d, carry):
        target = lax.rem(me + d, 32)
        pltpu.make_async_remote_copy(
            src_ref=routed_in.at[target], dst_ref=routed.at[me],
            send_sem=routed_s.at[d], recv_sem=routed_r.at[me],
            device_id=plane(target), device_id_type=MESH,
        ).start()
        return carry

    lax.fori_loop(1, 32, send_routed, 0)

    prod[:, 2 * HALF :, :] = jnp.zeros((2, 384 - 2 * HALF, 256), BF)
    for copy in loads:
        copy.wait()
    second_axis(0)
    wait_tok(0, 0, 3, 0)
    send_tok(tok.at[0, 0, 3, 0], (0, 0, 2, 0), plane(holder(0, 1, 0)))
    wait_tok(0, 0, 1, 1)
    send_tok(tok.at[0, 0, 1, 1], (0, 0, 2, 1), plane(holder(0, 3, 0)))
    wait_tok(0, 0, 1, 0)
    cross(0, 1)
    second_axis(1)
    wait_tok(0, 0, 3, 1)
    cross(0, 3)
    second_axis(3)

    def wait_routed(d, carry):
        source = lax.rem(me + d, 32)
        landed(routed.at[source], routed_r.at[source])
        return carry

    lax.fori_loop(1, 32, wait_routed, 0)
    for copy in weights:
        copy.wait()
    wait_tok(0, 0, 2, 0)
    wait_tok(0, 0, 2, 1)
    cross(0, 2)
    second_axis(2)

    def relay_tokens(da):
        wait_tok(0, 3, da, 0)
        send_tok(tok.at[0, 3, da, 0], (0, 2, da, 0), plane(holder(0, 0, 1)))
        wait_tok(0, 1, da, 1)
        send_tok(tok.at[0, 1, da, 1], (0, 2, da, 1), plane(holder(0, 0, 3)))
        wait_tok(0, 1, da, 0)
        cross(1, da)
        wait_tok(0, 3, da, 1)
        cross(3, da)

    def finish_tokens(da):
        wait_tok(0, 2, da, 0)
        wait_tok(0, 2, da, 1)
        cross(2, da)

    early = (
        lax.broadcasted_iota(jnp.int32, (128, 128), 0)
        < lax.broadcasted_iota(jnp.int32, (128, 128), 1)
    )
    early = jnp.where(early, 1.0, 0.0).astype(BF)
    row_of = lax.broadcasted_iota(jnp.int32, (HALF, 128), 0).astype(F32)
    outs = []

    def store(src, dst):
        copy = pltpu.make_async_copy(src, dst, out_s.at[len(outs)])
        copy.start()
        outs.append(copy)

    def gather(c):
        db = ORDER[c]
        for da in range(4):
            for arr in (0, 1):
                wait_tok(1, db, da, arr)
        for side in (0, 1):
            weight = jnp.zeros((HALF, 1), F32)
            for i in range(4):
                line = routed[holder(side, i, db)]
                member = line > 0
                rank = mm(jnp.where(member, 1.0, 0.0).astype(BF), early)
                target = jnp.where(member, rank + float(CAP * i), -1.0)
                hit = jnp.broadcast_to(target[0:1], (HALF, 128)) == row_of
                pick[:, i * 128 : (i + 1) * 128] = jnp.where(hit, 1.0, 0.0).astype(BF)
                weight += jnp.sum(
                    jnp.where(hit, jnp.broadcast_to(line[0:1], (HALF, 128)), 0.0),
                    axis=1, keepdims=True,
                )
            g_rows[c, side] = jnp.broadcast_to(weight, (HALF, 128))

            def columns(n, carry):
                cols = pl.ds(pl.multiple_of(n * 256, 256), 256)
                x = tok[side, db, :, 0, :, cols].reshape(512, 256)
                y = tok[side, db, :, 1, :, cols].reshape(512, 256)
                xr[c, side, :, cols] = mm(pick[...], x).astype(BF)
                rows = mm(pick[...], y)
                dyr[side, :, cols] = rows.astype(BF)
                g = g_rows[c, side]
                sdy[c, side, :, cols] = (rows * jnp.concatenate([g, g], axis=1)).astype(BF)
                return carry

            lax.fori_loop(0, 4, columns, 0)
        store(xr.at[c], xr_out.at[c])
        store(sdy.at[c], sdy_out.at[c])

    rs_sent = [[], [], [], []]

    def partial(c):
        p = c % 2
        if c >= 2:
            for copy in rs_sent[c - 2]:
                copy.wait_send()
        x_rows = xr.at[c]
        for rel in (2, 3, 1, 0):
            j = lax.rem(z + rel, 4)
            x = x_rows[...].reshape(2 * HALF, 1024)
            part[p, rel, :, 0] = mm(x, wg[j]).astype(BF).reshape(2, HALF, 256)
            part[p, rel, :, 1] = mm(x, wu[j]).astype(BF).reshape(2, HALF, 256)
            y = dyr[...].reshape(2 * HALF, 1024)
            part[p, rel, :, 2] = mm_nt(y, wd[j]).astype(BF).reshape(2, HALF, 256)
            if rel == 2:
                rs_sent[c] += [
                    send(part.at[p, 2, 0], r1.at[c, 0], r1_s.at[c, 0], r1_r.at[c, 0], column(3)),
                    send(part.at[p, 2, 1], r1.at[c, 1], r1_s.at[c, 1], r1_r.at[c, 1], column(1)),
                ]
            if rel == 3:
                rs_sent[c].append(send(
                    part.at[p, 3, 1], r2.at[c, 0, 1], r2_s.at[c, 0, 1], r2_r.at[c, 0, 1], column(3)
                ))
            if rel == 1:
                rs_sent[c].append(send(
                    part.at[p, 1, 0], r2.at[c, 1, 0], r2_s.at[c, 1, 0], r2_r.at[c, 1, 0], column(1)
                ))

    def add_on(c):
        p = c % 2
        for way, rel, half, step in ((0, 3, 0, 3), (1, 1, 1, 1)):
            landed(r1.at[c, way], r1_r.at[c, way])
            total = part[p, rel, half].astype(F32) + r1[c, way].astype(F32)
            part[p, rel, half] = total.astype(BF)
            rs_sent[c].append(send(
                part.at[p, rel, half], r2.at[c, way, half],
                r2_s.at[c, way, half], r2_r.at[c, way, half], column(step),
            ))

    def finish(c):
        p = c % 2
        for way in (0, 1):
            for half in (0, 1):
                landed(r2.at[c, way, half], r2_r.at[c, way, half])
        for half in (0, 1):

            def block(i, carry):
                rows = pl.ds(pl.multiple_of(i * 16, 16), 16)

                def total(arr):
                    return (
                        part[p, 0, half, arr, rows].astype(F32)
                        + r2[c, 0, half, arr, rows].astype(F32)
                        + r2[c, 1, half, arr, rows].astype(F32)
                    )

                gate_pre, up_pre, back = total(0), total(1), total(2)
                g = g_rows[c, half, rows]
                g = jnp.concatenate([g, g], axis=1)
                sig = jax.nn.sigmoid(gate_pre)
                swish = gate_pre * sig
                hidden = (swish * up_pre).astype(BF)
                product = back * hidden.astype(F32)
                grad_hidden = g * back
                slope = sig * (1.0 + gate_pre * (1.0 - sig))
                act[c, 0, half, 0, rows] = hidden
                act[c, 0, half, 1, rows] = (grad_hidden * up_pre * slope).astype(BF)
                act[c, 0, half, 2, rows] = (grad_hidden * swish).astype(BF)
                high = product.astype(BF)
                at = pl.ds(pl.multiple_of(half * HALF + i * 16, 16), 16)
                prod[0, at] = high
                prod[1, at] = (product - high.astype(F32)).astype(BF)
                return carry

            lax.fori_loop(0, HALF // 16, block, 0)
        for half in (0, 1):
            sent.append(send(
                act.at[c, 0, half], act.at[c, 3, half],
                ag_s.at[c, half], ag_r.at[c, 3, half], column(1),
            ))
            sent.append(send(
                act.at[c, 0, 1 - half], act.at[c, 1, 1 - half],
                ag_s.at[c, 3 - half], ag_r.at[c, 1, 1 - half], column(3),
            ))
        ones = jnp.ones((8, 256), BF)
        gates[c, 0] = mm_nt(ones, prod[0]) + mm_nt(ones, prod[1])
        for step in (1, 2, 3):
            sent.append(send(
                gates.at[c, 0], gates.at[c, 4 - step],
                gates_s.at[c, step], gates_r.at[c, 4 - step], column(step),
            ))
        store(act.at[c, 0], act_out.at[z, c])

    def relay(c):
        landed(act.at[c, 3, 0], ag_r.at[c, 3, 0])
        sent.append(send(
            act.at[c, 3, 0], act.at[c, 2, 0], ag_s.at[c, 4], ag_r.at[c, 2, 0], column(1)
        ))
        landed(act.at[c, 1, 1], ag_r.at[c, 1, 1])
        sent.append(send(
            act.at[c, 1, 1], act.at[c, 2, 1], ag_s.at[c, 5], ag_r.at[c, 2, 1], column(3)
        ))

    lane = lax.broadcasted_iota(jnp.int32, (PAD, HALF), 1)
    sub = lax.broadcasted_iota(jnp.int32, (PAD, HALF), 0)
    spread = jnp.concatenate(
        [
            jnp.where((lane == sub + CAP * i) & (sub < CAP), 1.0, 0.0)
            for i in range(4)
        ],
        axis=0,
    ).astype(BF)
    back_copies = []

    def give_back(c):
        for rel, half in ((3, 1), (1, 0), (2, 0), (2, 1)):
            landed(act.at[c, rel, half], ag_r.at[c, rel, half])
        for rel in (1, 2, 3):
            landed(gates.at[c, rel], gates_r.at[c, rel])
            store(act.at[c, rel], act_out.at[lax.rem(z + rel, 4), c])

        def columns(n, carry):
            at = pl.ds(pl.multiple_of(n * 256, 256), 256)
            total = jnp.zeros((2 * HALF, 256), F32)
            for rel in range(4):
                j = lax.rem(z + rel, 4)
                gate = act[c, rel, :, 1].reshape(2 * HALF, 256)
                up = act[c, rel, :, 2].reshape(2 * HALF, 256)
                total += mm_nt(gate, wg[j, at]) + mm_nt(up, wu[j, at])
            inp[:, :, at] = total.astype(BF).reshape(2, HALF, 256)
            return carry

        lax.fori_loop(0, 4, columns, 0)
        level = lax.broadcasted_iota(jnp.int32, (8, 384), 0)
        lines = jnp.zeros((8, 384), F32)
        for rel in range(4):
            lines = jnp.where(level == 4 + rel, gates[c, rel], lines)
        mask = lax.broadcasted_iota(jnp.int32, (8, 128), 1) < CAP
        for half in (0, 1):
            for n in range(4):
                at = pl.ds(n * 256, 256)
                wide = mm(spread, inp[half, :, at])
                for i in range(4):
                    k = half * 4 + i
                    block = wide[PAD * i : PAD * (i + 1)]
                    if n == 0:
                        turn = (384 - CAP * k) % 384
                        line = pltpu.roll(lines, turn, 1) if turn else lines
                        line = jnp.where(mask, line[:, :128], 0.0)
                        line = jnp.concatenate([line, jnp.zeros((8, 128), F32)], axis=1)
                        block = jnp.concatenate([block[:32], block[32:] + line], axis=0)
                    ret[c, k, :, at] = block.astype(BF)
            for i in range(4):
                k = half * 4 + i
                if c == 0 and k == 0:
                    store(ret.at[c, k], ret_out.at[me])
                else:
                    sent.append(send(
                        ret.at[c, k], ret_out.at[me], ret_s.at[c, k], ret_r.at[me],
                        plane(holder(half, i, ORDER[c])),
                    ))

    gather(0)
    partial(0)
    relay_tokens(0)
    add_on(0)
    relay_tokens(1)
    finish(0)
    relay_tokens(3)
    relay(0)
    relay_tokens(2)
    gather(1)
    partial(1)
    finish_tokens(0)
    finish_tokens(1)
    add_on(1)
    finish_tokens(3)
    finish_tokens(2)
    gather(2)
    partial(2)
    give_back(0)
    finish(1)
    add_on(2)
    relay(1)
    gather(3)
    partial(3)
    finish(2)
    add_on(3)
    relay(2)
    give_back(1)
    finish(3)
    give_back(2)
    relay(3)
    give_back(3)

    def wait_back(d, carry):
        source = lax.rem(me + d, 32)
        landed(ret_out.at[source], ret_r.at[source])
        return carry

    lax.fori_loop(1, 32, wait_back, 0)

    def wait_routed_sent(d, carry):
        target = lax.rem(me + d, 32)
        pltpu.make_async_copy(routed_in.at[target], routed_in.at[target], routed_s.at[d]).wait()
        return carry

    lax.fori_loop(1, 32, wait_routed_sent, 0)
    for copy in rs_sent[2] + rs_sent[3] + sent:
        copy.wait_send()
    for copy in outs:
        copy.wait()


def layer(tokens, cotangent, routed, wg, wu, wd):
    any_space = pl.BlockSpec(memory_space=pl.ANY)
    dma = pltpu.SemaphoreType.DMA
    vmem = pltpu.VMEM
    return pl.pallas_call(
        layer_kernel,
        out_shape=(
            jax.ShapeDtypeStruct((4, 2, HALF, 1024), BF),
            jax.ShapeDtypeStruct((4, 2, HALF, 1024), BF),
            jax.ShapeDtypeStruct((4, 4, 2, 3, HALF, 256), BF),
            jax.ShapeDtypeStruct((EXPERTS, PAD, 1024), BF),
        ),
        in_specs=[any_space] * 6,
        out_specs=(any_space,) * 4,
        scratch_shapes=[
            vmem((2, 4, 4, 2, 128, 1024), BF),
            vmem((4, 1024, 256), BF),
            vmem((4, 1024, 256), BF),
            vmem((4, 256, 1024), BF),
            vmem((EXPERTS, 8, 128), F32),
            vmem((HALF, 512), BF),
            vmem((4, 2, HALF, 128), F32),
            vmem((4, 2, HALF, 1024), BF),
            vmem((4, 2, HALF, 1024), BF),
            vmem((2, HALF, 1024), BF),
            vmem((2, 4, 2, 3, HALF, 256), BF),
            vmem((4, 2, 3, HALF, 256), BF),
            vmem((4, 2, 2, 3, HALF, 256), BF),
            vmem((4, 4, 2, 3, HALF, 256), BF),
            vmem((2, 384, 256), BF),
            vmem((4, 4, 8, 384), F32),
            vmem((2, HALF, 1024), BF),
            vmem((4, 8, PAD, 1024), BF),
            dma((15,)),
            dma((62,)),
            dma((2, 4, 4, 2)),
            dma((EXPERTS,)),
            dma((EXPERTS,)),
            dma((4, 2)),
            dma((4, 2)),
            dma((4, 2, 2)),
            dma((4, 2, 2)),
            dma((4, 6)),
            dma((4, 4, 2)),
            dma((4, 4)),
            dma((4, 4)),
            dma((4, 8)),
            dma((EXPERTS,)),
            dma((25,)),
        ],
        compiler_params=pltpu.CompilerParams(
            collective_id=0, has_side_effects=True, vmem_limit_bytes=67043328
        ),
        name="layer",
    )(tokens, cotangent, routed, wg, wu, wd)


def weights_kernel(xr_ref, sdy_ref, act_ref, gate_ref, up_ref, down_ref):
    rows = 8 * HALF
    hidden = act_ref[0, :, :, 0].reshape(rows, 256)
    gate = act_ref[0, :, :, 1].reshape(rows, 256)
    up = act_ref[0, :, :, 2].reshape(rows, 256)
    for n in range(4):
        at = pl.ds(n * 256, 256)
        x = xr_ref[:, :, :, at].reshape(rows, 256)
        y = sdy_ref[:, :, :, at].reshape(rows, 256)
        gate_ref[at, :] = mm_tn(x, gate)
        up_ref[at, :] = mm_tn(x, up)
        down_ref[:, at] = mm_tn(hidden, y)


def weight_grads(xr, sdy, act):
    whole = pl.BlockSpec((4, 2, HALF, 1024), lambda j: (0, 0, 0, 0))
    out = jax.ShapeDtypeStruct((1024, 1024), F32)
    return pl.pallas_call(
        weights_kernel,
        grid=(4,),
        out_shape=(out, out, out),
        in_specs=[
            whole,
            whole,
            pl.BlockSpec((1, 4, 2, 3, HALF, 256), lambda j: (j, 0, 0, 0, 0, 0)),
        ],
        out_specs=(
            pl.BlockSpec((1024, 256), lambda j: (0, j)),
            pl.BlockSpec((1024, 256), lambda j: (0, j)),
            pl.BlockSpec((256, 1024), lambda j: (j, 0)),
        ),
        compiler_params=pltpu.CompilerParams(vmem_limit_bytes=60000000),
        name="weight_grads",
    )(xr, sdy, act)


def shards(tokens, cotangent, gate_probs, expert_ids, gate_weight, up_weight, down_weight):
    count, width = tokens.shape
    wg, wu, wd = gate_weight[0], up_weight[0], down_weight[0]
    columns = jnp.arange(EXPERTS, dtype=jnp.int32)
    chosen = expert_ids[:, :, None] == columns[None, None, :]
    local = jnp.sum(jnp.where(chosen, gate_probs[:, :, None].astype(F32), 0.0), axis=1)
    routed = jnp.broadcast_to(local.T[:, None, :], (EXPERTS, 8, count))
    xr, sdy, act, ret = layer(tokens, cotangent, routed, wg, wu, wd)
    grad_gate, grad_up, grad_down = weight_grads(xr, sdy, act)
    before = (jnp.arange(count)[:, None] < jnp.arange(count)[None, :]).astype(BF)
    slots = jnp.arange(PAD, dtype=F32)
    local_rank = dot32("tu,te->ue", before, (local > 0).astype(BF))
    place = (local_rank[:, :, None] == slots[None, None, :]) & (local[:, :, None] > 0)
    gate_table = jnp.sum(ret[:, CAP:, :PAD].astype(F32), axis=1)
    by_expert = jnp.sum(jnp.where(place, gate_table[None], 0.0), axis=2)
    grad_gates = jnp.sum(jnp.where(chosen, by_expert[:, None, :], 0.0), axis=2)
    place = place.astype(BF).reshape(count, EXPERTS * PAD)
    grad_tokens = dot32("tr,rd->td", place, ret.reshape(EXPERTS * PAD, width)).astype(BF)
    return (grad_tokens, grad_gates, grad_gate[None], grad_up[None], grad_down[None])


def solution(mesh):
    placed = (
        P("expert", "dp"),
        P("expert", "dp"),
        P("expert", None),
        P("expert", None),
        P("expert", "dp", None),
        P("expert", "dp", None),
        P("expert", None, "dp"),
    )
    return jax.shard_map(
        shards,
        mesh=mesh,
        in_specs=placed,
        out_specs=(
            P("expert", "dp"),
            P("expert", None),
            P("expert", "dp", None),
            P("expert", "dp", None),
            P("expert", None, "dp"),
        ),
        check_vma=False,
    )
```

time: 353 us -> 196 us (0.56)
  waiting for transfers between devices: 218 us -> 0 us
  Pallas kernels: 0 us -> 187 us
  matrix products: 67.1 us -> 3.8 us
  starting transfers between devices: 19.1 us -> 0 us
  between operations: 14.3 us -> 0.7 us
  local copies, waits for them, and re-layouts: 13.4 us -> 1.27 us
  blocking collectives: 9.05 us -> 0 us
  other arithmetic: 9.98 us -> 3.26 us
    pallas_call x0 -> x2, Pallas kernels: none -> 187 us  [the longest x1 174 us: layer(): pl.pallas_call(layer_kernel, out_shape=(jax.ShapeDtypeStruct((4, 2, HALF,...]
    all_gather x4 -> x0, waiting for transfers between devices: 132 us -> none  [the longest x1 78.5 us: shards(): lax.all_gather(jnp.concatenate([tokens, cotangent, routed], axis=1), 'exp...]
    reduce_scatter x3 -> x0, waiting for transfers between devices: 77.2 us -> none  [shards(): lax.psum_scatter(part, 'dp', scatter_dimension=1, tiled=True)]
    dot_general x13 -> x2, matrix products: 67.1 us -> 3.8 us  [dot32(): return jnp.einsum(spec, a, b, preferred_element_type=F32)]
    all_to_all x2 -> x0, starting transfers between devices: 18.8 us -> none  [the longest x1 10.4 us: shards(): lax.all_to_all(gate_blocks.reshape(groups, CAP, -1), 'expert', split_axis...]
    reshape x5 -> x0, local copies, waits for them, and re-layouts: 13 us -> none  [the longest x1 4.1 us: shards(): dot32('gst,gtd->gsd', pick, x_all).astype(jnp.bfloat16).reshape(rows, width)]
    all_gather x1 -> x0, blocking collectives: 9.05 us -> none  [shards(): lax.all_gather(part, 'dp', axis=1, tiled=True)]
    all_to_all x2 -> x0, waiting for transfers between devices: 6.93 us -> none  [the longest x1 6.93 us: shards(): lax.all_to_all(input_part.reshape(groups, CAP, width), 'expert', split_ax...]
  transfers between devices with their start and end apart: 9 -> 0, of which waited for: 8 -> 0; matrix products, arithmetic and copies ran while one was open for 18% -> 0% of each run, Pallas kernels for 0% -> 0%
where the time goes in v2:
time: 196 us
  Pallas kernels  187 us (95%)
  matrix products  3.8 us (2%)
  other arithmetic  3.26 us (2%)
    pallas_call x1, Pallas kernels, layer(): pl.pallas_call(layer_kernel, out_shape=(jax.ShapeDtypeStruct((4, 2, HALF,...  174 us
    pallas_call x1, Pallas kernels, weight_grads(): pl.pallas_call(weights_kernel, grid=(4,), out_shape=(out, out, out), in_s...  13.2 us

profile of v2, /device:TPU:1, one launch (start us, length us, event | category | flops | bytes accessed | tf_op | source)
XLA Modules:
  0.0 196.0 jit_solution(3639915798466051838)
XLA Ops:
  0.6 0.7 convert_element_type.13
  1.3 0.7 select_reduce_fusion.2
  2.0 0.0 copy-start.1
  2.1 0.6 copy-done.1
  2.6 0.7 fusion.5
  3.4 0.7 broadcast_in_dim.61.routed_in
  4.0 173.7 %layer.1 = (bf16[4,2,144,1024]{3,2,1,0:T(8,128)(2,1)}, bf16[4,2,144,1024]{3,2,1,0:T(8,128)(2,1)}, bf16[4,4,2,3,144,256]{5,4,3,2,1,0:T(8,128)(2,1)}, bf16[32,40,1024]{2,1,0:T(8,128)(2,1)}) custom-call(bf16[128,1024]{1,0:T(8,128)(2,1)} %tok_in.1, bf16[128,1024]{1,0:T(8,128)(2,1)} %cot_in.1, f32[32,8,128]{2,1,0:T(8,128)} %broadcast_in_dim.61.routed_in, ...), custom_call_target="tpu_custom_call" | custom-call | tf_op jit(solution)/shard_map/layer/pallas_call | solution.py:454
  177.7 0.0 copy-start
  177.8 0.0 copy-start.2
  177.8 0.0 copy-start.3
  177.8 0.9 convert_reduce_fusion
  178.7 3.1 %fusion = bf16[128,1024]{1,0:T(8,128)(2,1)} fusion(bf16[32,40,1024]{2,1,0:T(8,128)(2,1)} %get-tuple-element.12, f32[128,32]{0,1:T(8,128)} %fusion.5, pred[128,32]{0,1:T(8,128)(4,1)} %copy-done.1), kind=kOutput, calls=%fused_computation.1 | convolution fusion | flops 336003072 | bytes 2904064 | tf_op jit(solution)/shard_map/tr,rd->td/dot_general | solution.py:23
  181.8 0.0 copy-done
  181.8 0.0 copy-done.2
  181.8 0.3 select_reduce_fusion
  182.1 0.0 copy-done.3
  182.1 0.6 select_reduce_fusion.1
  182.7 13.2 %weight_grads.1 = (f32[1024,1024]{1,0:T(8,128)}, f32[1024,1024]{1,0:T(8,128)}, f32[1024,1024]{1,0:T(8,128)}) custom-call(bf16[4,2,144,1024]{3,2,1,0:T(8,128)(2,1)} %get-tuple-element.13.xr_ref, bf16[4,2,144,1024]{3,2,1,0:T(8,128)(2,1)} %get-tuple-element.14.sdy_ref, bf16[4,4,2,3,144,256]{5,4,3,2,1,0:T(8,128)(2,1)} %get-tuple-element.15.act_ref), custom_call_target="tpu_custom_call" | custom-call | tf_op jit(solution)/shard_map/weight_grads/pallas_call | solution.py:524
  (1 shorter events, 0.0 us)
Async XLA Ops:
  2.0 0.6 copy-start.1
  177.7 4.0 %copy-start = (f32[128,32]{0,1:T(8,128)S(1)}, f32[128,32]{0,1:T(8,128)}, u32[]{:S(2)}) copy-start(f32[128,32]{0,1:T(8,128)} %fusion.5) | copy-start | bytes 49156
  177.8 4.0 %copy-start.2 = (pred[128,32]{0,1:T(8,128)(4,1)S(1)}, pred[128,32]{0,1:T(8,128)(4,1)}, u32[]{:S(2)}) copy-start(pred[128,32]{0,1:T(8,128)(4,1)} %copy-done.1) | copy-start | bytes 12292
  177.8 4.3 %copy-start.3 = (s32[128,8]{0,1:T(8,128)S(1)}, s32[128,8]{0,1:T(8,128)}, u32[]{:S(2)}) copy-start(s32[128,8]{0,1:T(8,128)} %param.10) | copy-start | bytes 12292
